TPU v7x, 32 devices: a whole 2x2x4 slice. The times are simulated.
32 devices in a mesh: aux: 4 (over y, x), occ: 8 (over z, core).
Axes of the slice: x: 2, y: 2, z: 4, core: 2. Of those that a mesh axis runs over, the one named last changes fastest.
Arguments:
- three_index: bfloat16 [2048, 32, 256], P('aux', 'occ'), may hold values from -0.8984375 to 0.8984375
- pair_list: int32 [8, 6], replicated, may hold values from 0 to 7
- pair_counts: int32 [8], replicated, may hold values from 1 to 6, as said below
- domains: int32 [8, 256], replicated, may hold values from 0 to 2047
- pao_energy: float32 [2048], replicated, may hold values from 0.5 to 3
- occ_energy: float32 [32], replicated, may hold values from -2 to -0.3
Outputs:
- density: bfloat16 [2048, 32, 256], P('aux', 'occ')
- pair_energy: float32 [8, 6], P('occ')
Inputs may be any that keep to these rules, and one draw needn't show every extreme that they name: `pair_list`: slots at or past a block's count are unused. `pair_counts`: some block uses all 6 slots.
All inputs are finite; a program needn't handle non-finite values.
Results may differ from a plain program's by a relative error of at most 0.0031.
Values may be sent and summed in bfloat16 or wider, within the bound.
No kernel may reach another device: no remote copies, remote signals or barrier semaphores. Data moves between devices by JAX's collectives and lax.ppermute only.
A program may use at most 64 MiB of HBM per device.

v0:
```python
import functools

import jax
import jax.numpy as jnp
from jax import lax
from jax.experimental import pallas as pl
from jax.experimental.pallas import tpu as pltpu
from jax.sharding import PartitionSpec as P


LANES = 128
HALVES = 2


def levels_kernel(table, index, out):
    wanted = index[...]
    lane, row = wanted % LANES, wanted // LANES
    for col in range(wanted.shape[1] // LANES):
        cols = slice(col * LANES, (col + 1) * LANES)
        found = jnp.zeros((wanted.shape[0], LANES), jnp.float32)
        for r in range(table.shape[0]):
            line = jnp.broadcast_to(table[r : r + 1, :], found.shape)
            hit = jnp.take_along_axis(line, lane[:, cols], axis=1)
            found = jnp.where(row[:, cols] == r, hit, found)
        out[:, cols] = found


def slot_kernel(part_count, halves, first, flags, *refs):
    rows_t = refs[:part_count]
    row_denom, col_denom = refs[part_count : part_count + 2]
    rest = refs[part_count + 2 :]
    parts = [rest[h * part_count : (h + 1) * part_count] for h in range(halves)]
    rest = rest[halves * part_count :]
    acc_in = None
    if not first:
        acc_in, rest = rest[:part_count], rest[part_count:]
    accs, energy = rest[:part_count], rest[part_count]
    width = parts[0][0].shape[1]
    amplitudes, energy_sum = [], None
    for h in range(halves):
        integrals = None
        for p in range(part_count):
            term = jnp.dot(rows_t[p][...], parts[h][p][...], preferred_element_type=jnp.float32)
            integrals = term if integrals is None else integrals + term
        denom = row_denom[...] + col_denom[:, h * width : (h + 1) * width]
        amplitude = (integrals / denom).astype(jnp.bfloat16)
        energy_row = jnp.sum(amplitude.astype(jnp.float32) * integrals, axis=0, keepdims=True)
        energy_sum = energy_row if energy_sum is None else energy_sum + energy_row
        amplitudes.append(amplitude)
    energy[...] = energy_sum[None]
    times = flags[0].astype(jnp.float32)
    crossed = flags[1] != 0
    for j in range(part_count):
        other = (j + part_count // 2) % part_count
        term = None
        for h in range(halves):
            block = jnp.where(crossed, parts[h][other][...], parts[h][j][...])
            product = lax.dot_general(
                block, amplitudes[h], (((1,), (1,)), ((), ())), preferred_element_type=jnp.float32
            )
            term = product if term is None else term + product
        term = times * term
        if not first:
            term = acc_in[j][...] + term
        accs[j][...] = term.astype(accs[j].dtype)


def slot_call(flags, rows_t, row_denom, col_denom, parts, accs, last):
    halves, part_count = len(parts), len(parts[0])
    depth, width = parts[0][0].shape
    rows = rows_t.shape[0]
    block = min(256, rows)
    first = accs is None

    def row_map(p):
        return lambda r, f: (r, (p + f[1] * (part_count // 2)) % part_count)

    acc_spec = pl.BlockSpec((depth, block), lambda r, f: (0, r))
    in_specs = [pl.BlockSpec((block, depth), row_map(p)) for p in range(part_count)]
    in_specs += [
        pl.BlockSpec((block, 1), lambda r, f: (r, 0)),
        pl.BlockSpec((1, halves * width), lambda r, f: (0, 0)),
    ]
    in_specs += [pl.BlockSpec((depth, width), lambda r, f: (0, 0))] * (halves * part_count)
    operands = [rows_t] * part_count + [row_denom, col_denom] + [part for half in parts for part in half]
    aliases = {}
    if not first:
        in_specs += [acc_spec] * part_count
        if not last:
            aliases = {1 + len(operands) + p: p for p in range(part_count)}
        operands += list(accs)
    kinds = [jnp.float32] * part_count
    if last:
        kinds = [jnp.float32] + [jnp.bfloat16] * (part_count - 1)
    outs = pl.pallas_call(
        functools.partial(slot_kernel, part_count, halves, first),
        grid_spec=pltpu.PrefetchScalarGridSpec(
            num_scalar_prefetch=1,
            grid=(rows // block,),
            in_specs=in_specs,
            out_specs=[acc_spec] * part_count + [pl.BlockSpec((1, 1, width), lambda r, f: (r, 0, 0))],
        ),
        out_shape=[jax.ShapeDtypeStruct((depth, rows), kind) for kind in kinds]
        + [jax.ShapeDtypeStruct((rows // block, 1, width), jnp.float32)],
        input_output_aliases=aliases,
        compiler_params=pltpu.CompilerParams(vmem_limit_bytes=56 * 1024 * 1024),
        cost_estimate=pl.CostEstimate(
            flops=4 * rows * halves * width * depth * part_count,
            bytes_accessed=2 * part_count * depth * (halves * width + rows) + 8 * part_count * depth * rows,
            transcendentals=0,
        ),
        name="slot",
    )(flags, *operands)
    return outs[:part_count], jnp.sum(outs[part_count])


def per_device(three_index, pair_list, pair_counts, domains, pao_energy, occ_energy):
    aux_local, occ_dev, dom_width = three_index.shape
    pair_rows = occ_dev * dom_width
    width = pair_rows // HALVES
    block_count = lax.axis_size("occ")
    block_id = lax.axis_index("occ")
    aux_count = lax.axis_size("aux")
    aux_rank = lax.axis_index("aux")
    slot_total = pair_list.shape[1]
    layers = block_count // 2
    rings = aux_count // 2
    rows = pair_rows // rings
    layer, core = block_id // 2, block_id % 2
    ring, side = aux_rank // 2, aux_rank % 2
    crossed = (core != side).astype(jnp.int32)
    axes = ("aux", "occ")

    def flat(y, x, z, c):
        return (y * 2 + x) * block_count + z * 2 + c

    everyone = [
        (y, x, z, c) for y in range(rings) for x in range(2) for z in range(layers) for c in range(2)
    ]
    swap = [
        (flat(y, x, z, c), flat(y, x, z, c) if c == x else flat(y, 1 - x, z, 1 - c)) for y, x, z, c in everyone
    ]
    lend = [(flat(y, x, z, c), flat(y, x, z, c) if c == x else flat(y, 1 - x, z, 1 - c)) for y, x, z, c in everyone]
    down = [(i, (i - 2) % block_count) for i in range(block_count)]
    other_core = [(i, i ^ 1) for i in range(block_count)]

    def to_chip(dy, dx):
        return [(y * 2 + x, ((y + dy) % rings) * 2 + (x ^ dx)) for y in range(rings) for x in range(2)]

    halves = range(HALVES)
    own_block = [
        three_index[:, h * occ_dev // HALVES : (h + 1) * occ_dev // HALVES].reshape(aux_local, width) for h in halves
    ]
    held = [[lax.ppermute(own_block[h], axes, swap) for h in halves]]
    for k in range(1, layers):
        held.append([lax.ppermute(held[k - 1][h], "occ", down) for h in halves])
    turned = []
    for k in range(layers):
        turned.append([])
        for h in halves:
            if k == layers - 1 and h == HALVES - 1:
                turned[k].append([lax.ppermute(part, "occ", down) for part in turned[k - 1][h]])
            else:
                turned[k].append([lax.ppermute(held[k][h], "aux", to_chip(-dy, 0)) for dy in range(1, rings)])

    def all_parts(k, h):
        mine = [held[k][h]] + turned[k][h]
        return mine + [lax.ppermute(part, "occ", other_core) for part in mine]

    levels = pl.pallas_call(
        levels_kernel, out_shape=jax.ShapeDtypeStruct(domains.shape, jnp.float32), name="levels"
    )(pao_energy.reshape(-1, LANES), domains)
    occ_levels = occ_energy.reshape(block_count, occ_dev)
    denoms = (levels[:, None, :] - occ_levels[:, :, None]).reshape(block_count, pair_rows)
    row_denom = lax.dynamic_slice(denoms, (block_id, ring * rows), (1, rows)).reshape(rows, 1)
    my_pairs = pair_list[block_id]
    valid = jnp.arange(slot_total, dtype=jnp.int32) < pair_counts[block_id]

    energies = jnp.zeros((slot_total,), jnp.float32)
    accs = None
    rows_t = None
    for k in range(layers):
        parts = [all_parts(k, h) for h in halves]
        if k == 0:
            start = ring * rows
            local = jnp.concatenate(
                [
                    lax.dynamic_slice(
                        jnp.where(start < width, parts[0][p], parts[1][p]), (0, start % width), (aux_local, rows)
                    )
                    for p in range(aux_count)
                ],
                axis=0,
            )
            rows_t = lax.ppermute(local, axes, lend).T
        partner_id = 2 * ((layer + k) % layers) + side
        hits = (my_pairs == partner_id) & valid
        flags = jnp.stack([jnp.sum(hits.astype(jnp.int32)), crossed])
        col_denom = lax.dynamic_slice(denoms, (partner_id, 0), (1, pair_rows))
        if k < layers - 1:
            steps = [(parts, col_denom)]
        else:
            steps = [([parts[h]], col_denom[:, h * width : (h + 1) * width]) for h in halves]
        for i, (step_parts, step_denom) in enumerate(steps):
            last = k == layers - 1 and i == len(steps) - 1
            accs, energy = slot_call(flags, rows_t, row_denom, step_denom, step_parts, accs, last)
            energies = energies + jnp.where(hits, energy / (pair_rows * pair_rows), 0.0)

    slices = []
    for dy in range(rings):
        near, far = accs[dy], lax.ppermute(accs[rings + dy], "aux", to_chip(dy, 1))
        if dy > 0:
            near = lax.ppermute(near, "aux", to_chip(dy, 0))
        slices.append((near.astype(jnp.float32) + far.astype(jnp.float32)).astype(jnp.bfloat16))
    energies = lax.psum(energies, "aux")
    ordered = []
    for i in range(rings):
        chosen = slices[0]
        for dy in range(1, rings):
            chosen = jnp.where((ring - i) % rings == dy, slices[dy], chosen)
        ordered.append(chosen)
    density_out = jnp.concatenate(ordered, axis=1)
    return (density_out.reshape(aux_local, occ_dev, dom_width), energies[None])


def solution(mesh):
    placed = (P("aux", "occ", None), P(), P(), P(), P(), P())

    return jax.shard_map(
        per_device,
        mesh=mesh,
        in_specs=placed,
        out_specs=(P("aux", "occ", None), P("occ", None)),
        check_vma=False,
    )
```

profile of v0, /device:TPU:0, one launch (start us, length us, event | category | flops | bytes accessed | tf_op | source)
XLA Modules:
  0.0 189.0 jit_solution(9150012512330011289)
XLA Ops:
  0.6 2.4 %fusion = (bf16[512,2,256]{2,1,0:T(2,128)(2,1)S(1)}, bf16[512,2,256]{2,1,0:T(2,128)(2,1)S(1)}) fusion(bf16[512,4,256]{2,1,0:T(4,128)(2,1)} %param.6), kind=kLoop, calls=%fused_computation.31 | loop fusion | bytes 2097152 | tf_op jit(solution)/shard_map/slice | solution.py:152
  7.9 3.0 %collective-permute-start.2 = (bf16[512,512]{1,0:T(8,128)(2,1)}, bf16[512,512]{1,0:T(8,128)(2,1)S(1)}, u32[]{:S(2)}, u32[]{:S(2)}) collective-permute-start(bf16[512,512]{1,0:T(8,128)(2,1)} %collective-permute-done.refs_6_), channel_id=1, source_target_pairs={{0,16},{8,24},{16,0},{24,8},{1,17},{9,25},{17,1},{25,9},{2,18},{10... | collective-permute-start | bytes 1572872 | tf_op jit(solution)/shard_map/ppermute | solution.py:164
  11.0 12.0 %collective-permute-start.4 = (bf16[512,512]{1,0:T(8,128)(2,1)}, bf16[512,512]{1,0:T(8,128)(2,1)S(1)}, u32[]{:S(2)}, u32[]{:S(2)}) collective-permute-start(bf16[512,512]{1,0:T(8,128)(2,1)} %collective-permute-done.refs_6_), channel_id=1, source_target_pairs={{0,1},{1,0},{2,3},{3,2},{4,5},{5,4},{6,7},{7,6},{8,9},{9,8},{10,11... | collective-permute-start | bytes 1572872 | tf_op jit(solution)/shard_map/ppermute | solution.py:168
  23.0 3.6 %collective-permute-start.16 = (bf16[512,512]{1,0:T(8,128)(2,1)}, bf16[512,512]{1,0:T(8,128)(2,1)S(1)}, u32[]{:S(2)}, u32[]{:S(2)}) collective-permute-start(bf16[512,512]{1,0:T(8,128)(2,1)} %collective-permute-done.refs_6_), channel_id=1, source_target_pairs={{0,6},{1,7},{2,0},{3,1},{4,2},{5,3},{6,4},{7,5},{8,14},{9,15},{10,... | collective-permute-start | bytes 1572872 | tf_op jit(solution)/shard_map/ppermute | solution.py:156
  27.8 1.8 collective-permute-start.6
  29.7 5.6 %collective-permute-start.7 = (bf16[512,512]{1,0:T(8,128)(2,1)S(1)}, bf16[512,512]{1,0:T(8,128)(2,1)S(1)}, u32[]{:S(2)}, u32[]{:S(2)}) collective-permute-start(bf16[512,512]{1,0:T(8,128)(2,1)S(1)} %collective-permute-done.3.refs_11_), channel_id=1, source_target_pairs={{0,1},{1,0},{2,3},{3,2},{4,5},{5,4},{6,7},{7,6},{8,9},{9,8},{10,11... | collective-permute-start | bytes 1572872 | tf_op jit(solution)/shard_map/ppermute | solution.py:168
  35.3 4.2 %collective-permute-start.9 = (bf16[512,512]{1,0:T(8,128)(2,1)}, bf16[512,512]{1,0:T(8,128)(2,1)S(1)}, u32[]{:S(2)}, u32[]{:S(2)}) collective-permute-start(bf16[512,512]{1,0:T(8,128)(2,1)} %collective-permute-done.1.refs_10_), channel_id=1, source_target_pairs={{0,6},{1,7},{2,0},{3,1},{4,2},{5,3},{6,4},{7,5},{8,14},{9,15},{10,... | collective-permute-start | bytes 1572872 | tf_op jit(solution)/shard_map/ppermute | solution.py:156
  41.4 1.5 pad_maximum_fusion
  42.9 2.2 %collective-permute-start.8 = (bf16[2048,512]{1,0:T(8,128)(2,1)}, bf16[2048,512]{1,0:T(8,128)(2,1)S(1)}, u32[]{:S(2)}, u32[]{:S(2)}) collective-permute-start(bf16[2048,512]{1,0:T(8,128)(2,1)} %pad_maximum_fusion), channel_id=1, source_target_pairs={{0,0},{1,8},{2,2},{3,10},{4,4},{5,12},{6,6},{7,14},{8,1},{9,9},{10... | collective-permute-start | bytes 6291464 | tf_op jit(solution)/shard_map/ppermute | solution.py:195
  45.1 1.5 collective-permute-start.27
  46.6 4.5 %collective-permute-done.9.refs_10_ = bf16[512,512]{1,0:T(8,128)(2,1)S(1)} collective-permute-done((bf16[512,512]{1,0:T(8,128)(2,1)}, bf16[512,512]{1,0:T(8,128)(2,1)S(1)}, u32[]{:S(2)}, u32[]{:S(2)}) %collective-permute-start.9) | collective-permute-done | bytes 524320 | tf_op jit(solution)/shard_map/ppermute | solution.py:156
  51.2 1.5 collective-permute-start.30
  53.2 6.8 %collective-permute-done.27.refs_7_ = bf16[512,512]{1,0:T(8,128)(2,1)} collective-permute-done((bf16[512,512]{1,0:T(8,128)(2,1)S(1)}, bf16[512,512]{1,0:T(8,128)(2,1)}, u32[]{:S(2)}, u32[]{:S(2)}) %collective-permute-start.27) | collective-permute-done | bytes 524320 | tf_op jit(solution)/shard_map/ppermute | solution.py:164
  60.5 9.9 %collective-permute-done.30.refs_11_ = bf16[512,512]{1,0:T(8,128)(2,1)} collective-permute-done((bf16[512,512]{1,0:T(8,128)(2,1)S(1)}, bf16[512,512]{1,0:T(8,128)(2,1)}, u32[]{:S(2)}, u32[]{:S(2)}) %collective-permute-start.30) | collective-permute-done | bytes 524320 | tf_op jit(solution)/shard_map/ppermute | solution.py:164
  72.3 1.5 collective-permute-start.12
  76.0 2.1 %convert_reduce_fusion = (s32[]{:T(128)}, s32[]{:T(128)}, s32[]{:T(128)}, s32[]{:T(128)}, s32[1,6]{1,0:T(1,128)S(1)}) fusion(s32[]{:T(128)} %bitcast.1, s32[]{:T(128)S(6)} %add.115, s32[]{:T(128)S(6)} %add.112, s32[]{:T(128)S(6)} %add.108, s32[]{:T(128)S(6)} %add.102, s32[8,6]{1,0:T(8,128)} %param.7, s32[]{:T(128)S(6)} %select_n.125), kind=kLoop, calls=%fused_computation.26 | loop fusion | flops 98 | bytes 88 | tf_op jit(solution)/shard_map/reduce_sum | solution.py:198
  79.3 4.3 %collective-permute-done.17.refs_6_ = bf16[512,512]{1,0:T(8,128)(2,1)} collective-permute-done((bf16[512,512]{1,0:T(8,128)(2,1)S(1)}, bf16[512,512]{1,0:T(8,128)(2,1)}, u32[]{:S(2)}, u32[]{:S(2)}) %collective-permute-start.17) | collective-permute-done | bytes 524320 | tf_op jit(solution)/shard_map/ppermute | solution.py:156
  83.6 3.0 %collective-permute-start.18 = (bf16[512,512]{1,0:T(8,128)(2,1)}, bf16[512,512]{1,0:T(8,128)(2,1)}, u32[]{:S(2)}, u32[]{:S(2)}) collective-permute-start(bf16[512,512]{1,0:T(8,128)(2,1)} %collective-permute-done.17.refs_6_), channel_id=1, source_target_pairs={{0,6},{1,7},{2,0},{3,1},{4,2},{5,3},{6,4},{7,5},{8,14},{9,15},{10,... | collective-permute-start | bytes 1572872 | tf_op jit(solution)/shard_map/ppermute | solution.py:156
  89.1 1.5 collective-permute-start.22
  92.6 4.4 %collective-permute-done.18.refs_6_ = bf16[512,512]{1,0:T(8,128)(2,1)} collective-permute-done((bf16[512,512]{1,0:T(8,128)(2,1)}, bf16[512,512]{1,0:T(8,128)(2,1)}, u32[]{:S(2)}, u32[]{:S(2)}) %collective-permute-start.18) | collective-permute-done | bytes 524320 | tf_op jit(solution)/shard_map/ppermute | solution.py:156
  97.0 4.3 %collective-permute-start.11 = (bf16[512,512]{1,0:T(8,128)(2,1)}, bf16[512,512]{1,0:T(8,128)(2,1)}, u32[]{:S(2)}, u32[]{:S(2)}) collective-permute-start(bf16[512,512]{1,0:T(8,128)(2,1)} %collective-permute-done.10.refs_10_), channel_id=1, source_target_pairs={{0,6},{1,7},{2,0},{3,1},{4,2},{5,3},{6,4},{7,5},{8,14},{9,15},{10,... | collective-permute-start | bytes 1572872 | tf_op jit(solution)/shard_map/ppermute | solution.py:156
  101.3 1.5 collective-permute-start.19
  105.5 2.4 %copy.66.refs_0_.refs_1_.refs_2_.refs_3_ = bf16[512,2048]{1,0:T(8,128)(2,1)} copy(bf16[512,2048]{0,1:T(8,128)(2,1)S(1)} %bitcast.39) | data formatting | bytes 4194304 | tf_op jit(solution)/shard_map/transpose | solution.py:195
  108.6 9.5 %slot.5 = (f32[512,512]{1,0:T(8,128)}, f32[512,512]{1,0:T(8,128)}, f32[512,512]{1,0:T(8,128)}, f32[512,512]{1,0:T(8,128)}, f32[2,1,512]{2,1,0:T(1,128)}) custom-call(s32[2]{0:T(128)} %pad_add_fusion.3.flags, bf16[512,2048]{1,0:T(8,128)(2,1)} %copy.66.refs_0_.refs_1_.refs_2_.refs_3_, bf16[512,2048]{1,0:T(8,128)(2,1)} %copy.66.refs_0_.refs_1_.refs_2_.refs_3_, ...), custom_call_target="tpu_custom_call" | custom-call | flops 4294967296 | bytes 14680064 | tf_op jit(solution)/shard_map/slot/pallas_call | solution.py:95
  118.7 10.0 %slot.6 = (f32[512,512]{1,0:T(8,128)}, f32[512,512]{1,0:T(8,128)}, f32[512,512]{1,0:T(8,128)}, f32[512,512]{1,0:T(8,128)}, f32[2,1,512]{2,1,0:T(1,128)}) custom-call(s32[2]{0:T(128)} %pad_add_fusion.2.flags, bf16[512,2048]{1,0:T(8,128)(2,1)} %copy.66.refs_0_.refs_1_.refs_2_.refs_3_, ...), custom_call_target="tpu_custom_call", output_to_operand_aliasing={{0}: (15, {}), {1}: (16, {}), {2}: (17, {}), {3}: (18, {})} | custom-call | flops 4294967296 | bytes 14680064 | tf_op jit(solution)/shard_map/slot/pallas_call | solution.py:95
  130.1 10.0 %slot.7 = (f32[512,512]{1,0:T(8,128)}, f32[512,512]{1,0:T(8,128)}, f32[512,512]{1,0:T(8,128)}, f32[512,512]{1,0:T(8,128)}, f32[2,1,512]{2,1,0:T(1,128)}) custom-call(s32[2]{0:T(128)} %pad_add_fusion.1.flags, bf16[512,2048]{1,0:T(8,128)(2,1)} %copy.66.refs_0_.refs_1_.refs_2_.refs_3_, ...), custom_call_target="tpu_custom_call", output_to_operand_aliasing={{0}: (15, {}), {1}: (16, {}), {2}: (17, {}), {3}: (18, {})} | custom-call | flops 4294967296 | bytes 14680064 | tf_op jit(solution)/shard_map/slot/pallas_call | solution.py:95
  141.1 7.3 %slot.8 = (f32[512,512]{1,0:T(8,128)}, f32[512,512]{1,0:T(8,128)}, f32[512,512]{1,0:T(8,128)}, f32[512,512]{1,0:T(8,128)}, f32[2,1,512]{2,1,0:T(1,128)}) custom-call(s32[2]{0:T(128)} %pad_add_fusion.flags, bf16[512,2048]{1,0:T(8,128)(2,1)} %copy.66.refs_0_.refs_1_.refs_2_.refs_3_, ...), custom_call_target="tpu_custom_call", output_to_operand_aliasing={{0}: (11, {}), {1}: (12, {}), {2}: (13, {}), {3}: (14, {})} | custom-call | flops 2147483648 | bytes 12582912 | tf_op jit(solution)/shard_map/slot/pallas_call | solution.py:95
  149.3 7.1 %slot.9 = (f32[512,512]{1,0:T(8,128)}, bf16[512,512]{1,0:T(8,128)(2,1)}, bf16[512,512]{1,0:T(8,128)(2,1)}, bf16[512,512]{1,0:T(8,128)(2,1)}, f32[2,1,512]{2,1,0:T(1,128)}) custom-call(s32[2]{0:T(128)} %pad_add_fusion.flags, bf16[512,2048]{1,0:T(8,128)(2,1)} %copy.66.refs_0_.refs_1_.refs_2_.refs_3_, bf16[512,2048]{1,0:T(8,128)(2,1)} %copy.66.refs_0_.refs_1_.refs_2_.refs_3_, ...), custom_call_target="tpu_custom_call" | custom-call | flops 2147483648 | bytes 12582912 | tf_op jit(solution)/shard_map/slot/pallas_call | solution.py:95
  157.0 3.0 %collective-permute-start.35 = (bf16[512,512]{1,0:T(8,128)(2,1)}, bf16[512,512]{1,0:T(8,128)(2,1)S(1)}, u32[]{:S(2)}, u32[]{:S(2)}) collective-permute-start(bf16[512,512]{1,0:T(8,128)(2,1)} %get-tuple-element.46), channel_id=1, source_target_pairs={{0,8},{8,0},{16,24},{24,16},{1,9},{9,1},{17,25},{25,17},{2,10},{10... | collective-permute-start | bytes 1572872 | tf_op jit(solution)/shard_map/ppermute | solution.py:211
  167.6 18.1 %psum.7 = f32[1,6]{1,0:T(1,128)} all-reduce(f32[1,6]{1,0:T(1,128)S(1)} %add_bitcast_fusion), channel_id=1, replica_groups=mesh['aux'=4,'occ'=8] {'aux'}, use_global_device_ids=true, to_apply=%region_9.10 | all-reduce | flops 6 | bytes 48 | tf_op jit(solution)/shard_map/psum | solution.py:215
  185.8 1.5 broadcast_select_fusion.5
  187.5 1.6 reshape.37
  (125 shorter events, 31.0 us)
Async XLA Ops:
  7.9 19.9 %collective-permute-start.2 = (bf16[512,512]{1,0:T(8,128)(2,1)}, bf16[512,512]{1,0:T(8,128)(2,1)S(1)}, u32[]{:S(2)}, u32[]{:S(2)}) collective-permute-start(bf16[512,512]{1,0:T(8,128)(2,1)} %collective-permute-done.refs_6_), channel_id=1, source_target_pairs={{0,16},{8,24},{16,0},{24,8},{1,17},{9,25},{17,1},{25,9},{2,18},{10... | collective-permute-start | bytes 1572872 | tf_op jit(solution)/shard_map/ppermute | solution.py:164
  10.9 18.7 %collective-permute-start.3 = (bf16[512,512]{1,0:T(8,128)(2,1)}, bf16[512,512]{1,0:T(8,128)(2,1)S(1)}, u32[]{:S(2)}, u32[]{:S(2)}) collective-permute-start(bf16[512,512]{1,0:T(8,128)(2,1)} %collective-permute-done.1.refs_10_), channel_id=1, source_target_pairs={{0,16},{8,24},{16,0},{24,8},{1,17},{9,25},{17,1},{25,9},{2,18},{10... | collective-permute-start | bytes 1572872 | tf_op jit(solution)/shard_map/ppermute | solution.py:164
  11.0 24.3 %collective-permute-start.4 = (bf16[512,512]{1,0:T(8,128)(2,1)}, bf16[512,512]{1,0:T(8,128)(2,1)S(1)}, u32[]{:S(2)}, u32[]{:S(2)}) collective-permute-start(bf16[512,512]{1,0:T(8,128)(2,1)} %collective-permute-done.refs_6_), channel_id=1, source_target_pairs={{0,1},{1,0},{2,3},{3,2},{4,5},{5,4},{6,7},{7,6},{8,9},{9,8},{10,11... | collective-permute-start | bytes 1572872 | tf_op jit(solution)/shard_map/ppermute | solution.py:168
  23.0 16.5 %collective-permute-start.5 = (bf16[512,512]{1,0:T(8,128)(2,1)}, bf16[512,512]{1,0:T(8,128)(2,1)S(1)}, u32[]{:S(2)}, u32[]{:S(2)}) collective-permute-start(bf16[512,512]{1,0:T(8,128)(2,1)} %collective-permute-done.1.refs_10_), channel_id=1, source_target_pairs={{0,1},{1,0},{2,3},{3,2},{4,5},{5,4},{6,7},{7,6},{8,9},{9,8},{10,11... | collective-permute-start | bytes 1572872 | tf_op jit(solution)/shard_map/ppermute | solution.py:168
  23.0 22.1 %collective-permute-start.16 = (bf16[512,512]{1,0:T(8,128)(2,1)}, bf16[512,512]{1,0:T(8,128)(2,1)S(1)}, u32[]{:S(2)}, u32[]{:S(2)}) collective-permute-start(bf16[512,512]{1,0:T(8,128)(2,1)} %collective-permute-done.refs_6_), channel_id=1, source_target_pairs={{0,6},{1,7},{2,0},{3,1},{4,2},{5,3},{6,4},{7,5},{8,14},{9,15},{10,... | collective-permute-start | bytes 1572872 | tf_op jit(solution)/shard_map/ppermute | solution.py:156
  35.3 15.8 %collective-permute-start.9 = (bf16[512,512]{1,0:T(8,128)(2,1)}, bf16[512,512]{1,0:T(8,128)(2,1)S(1)}, u32[]{:S(2)}, u32[]{:S(2)}) collective-permute-start(bf16[512,512]{1,0:T(8,128)(2,1)} %collective-permute-done.1.refs_10_), channel_id=1, source_target_pairs={{0,6},{1,7},{2,0},{3,1},{4,2},{5,3},{6,4},{7,5},{8,14},{9,15},{10,... | collective-permute-start | bytes 1572872 | tf_op jit(solution)/shard_map/ppermute | solution.py:156
  42.9 58.4 %collective-permute-start.8 = (bf16[2048,512]{1,0:T(8,128)(2,1)}, bf16[2048,512]{1,0:T(8,128)(2,1)S(1)}, u32[]{:S(2)}, u32[]{:S(2)}) collective-permute-start(bf16[2048,512]{1,0:T(8,128)(2,1)} %pad_maximum_fusion), channel_id=1, source_target_pairs={{0,0},{1,8},{2,2},{3,10},{4,4},{5,12},{6,6},{7,14},{8,1},{9,9},{10... | collective-permute-start | bytes 6291464 | tf_op jit(solution)/shard_map/ppermute | solution.py:195
  45.1 14.9 %collective-permute-start.27 = (bf16[512,512]{1,0:T(8,128)(2,1)S(1)}, bf16[512,512]{1,0:T(8,128)(2,1)}, u32[]{:S(2)}, u32[]{:S(2)}) collective-permute-start(bf16[512,512]{1,0:T(8,128)(2,1)S(1)} %collective-permute-done.16.refs_6_), channel_id=1, source_target_pairs={{0,16},{8,24},{16,0},{24,8},{1,17},{9,25},{17,1},{25,9},{2,18},{10... | collective-permute-start | bytes 1572872 | tf_op jit(solution)/shard_map/ppermute | solution.py:164
  51.2 19.2 %collective-permute-start.30 = (bf16[512,512]{1,0:T(8,128)(2,1)S(1)}, bf16[512,512]{1,0:T(8,128)(2,1)}, u32[]{:S(2)}, u32[]{:S(2)}) collective-permute-start(bf16[512,512]{1,0:T(8,128)(2,1)S(1)} %collective-permute-done.9.refs_10_), channel_id=1, source_target_pairs={{0,16},{8,24},{16,0},{24,8},{1,17},{9,25},{17,1},{25,9},{2,18},{10... | collective-permute-start | bytes 1572872 | tf_op jit(solution)/shard_map/ppermute | solution.py:164
  52.7 18.5 %collective-permute-start.28 = (bf16[512,512]{1,0:T(8,128)(2,1)S(1)}, bf16[512,512]{1,0:T(8,128)(2,1)S(1)}, u32[]{:S(2)}, u32[]{:S(2)}) collective-permute-start(bf16[512,512]{1,0:T(8,128)(2,1)S(1)} %collective-permute-done.16.refs_6_), channel_id=1, source_target_pairs={{0,1},{1,0},{2,3},{3,2},{4,5},{5,4},{6,7},{7,6},{8,9},{9,8},{10,11... | collective-permute-start | bytes 1572872 | tf_op jit(solution)/shard_map/ppermute | solution.py:168
  52.7 18.5 %collective-permute-start.31 = (bf16[512,512]{1,0:T(8,128)(2,1)S(1)}, bf16[512,512]{1,0:T(8,128)(2,1)S(1)}, u32[]{:S(2)}, u32[]{:S(2)}) collective-permute-start(bf16[512,512]{1,0:T(8,128)(2,1)S(1)} %collective-permute-done.9.refs_10_), channel_id=1, source_target_pairs={{0,1},{1,0},{2,3},{3,2},{4,5},{5,4},{6,7},{7,6},{8,9},{9,8},{10,11... | collective-permute-start | bytes 1572872 | tf_op jit(solution)/shard_map/ppermute | solution.py:168
  60.0 12.3 %collective-permute-start.10 = (bf16[512,512]{1,0:T(8,128)(2,1)S(1)}, bf16[512,512]{1,0:T(8,128)(2,1)}, u32[]{:S(2)}, u32[]{:S(2)}) collective-permute-start(bf16[512,512]{1,0:T(8,128)(2,1)S(1)} %collective-permute-done.9.refs_10_), channel_id=1, source_target_pairs={{0,6},{1,7},{2,0},{3,1},{4,2},{5,3},{6,4},{7,5},{8,14},{9,15},{10,... | collective-permute-start | bytes 1572872 | tf_op jit(solution)/shard_map/ppermute | solution.py:156
  70.4 13.2 %collective-permute-start.17 = (bf16[512,512]{1,0:T(8,128)(2,1)S(1)}, bf16[512,512]{1,0:T(8,128)(2,1)}, u32[]{:S(2)}, u32[]{:S(2)}) collective-permute-start(bf16[512,512]{1,0:T(8,128)(2,1)S(1)} %collective-permute-done.16.refs_6_), channel_id=1, source_target_pairs={{0,6},{1,7},{2,0},{3,1},{4,2},{5,3},{6,4},{7,5},{8,14},{9,15},{10,... | collective-permute-start | bytes 1572872 | tf_op jit(solution)/shard_map/ppermute | solution.py:156
  71.2 17.9 %collective-permute-start.29 = (bf16[512,512]{1,0:T(8,128)(2,1)}, bf16[512,512]{1,0:T(8,128)(2,1)}, u32[]{:S(2)}, u32[]{:S(2)}) collective-permute-start(bf16[512,512]{1,0:T(8,128)(2,1)} %collective-permute-done.27.refs_7_), channel_id=1, source_target_pairs={{0,1},{1,0},{2,3},{3,2},{4,5},{5,4},{6,7},{7,6},{8,9},{9,8},{10,11... | collective-permute-start | bytes 1572872 | tf_op jit(solution)/shard_map/ppermute | solution.py:168
  71.2 19.4 %collective-permute-start.32 = (bf16[512,512]{1,0:T(8,128)(2,1)}, bf16[512,512]{1,0:T(8,128)(2,1)}, u32[]{:S(2)}, u32[]{:S(2)}) collective-permute-start(bf16[512,512]{1,0:T(8,128)(2,1)} %collective-permute-done.30.refs_11_), channel_id=1, source_target_pairs={{0,1},{1,0},{2,3},{3,2},{4,5},{5,4},{6,7},{7,6},{8,9},{9,8},{10,11... | collective-permute-start | bytes 1572872 | tf_op jit(solution)/shard_map/ppermute | solution.py:168
  72.3 18.3 %collective-permute-start.12 = (bf16[512,512]{1,0:T(8,128)(2,1)}, bf16[512,512]{1,0:T(8,128)(2,1)}, u32[]{:S(2)}, u32[]{:S(2)}) collective-permute-start(bf16[512,512]{1,0:T(8,128)(2,1)} %collective-permute-done.10.refs_10_), channel_id=1, source_target_pairs={{0,16},{8,24},{16,0},{24,8},{1,17},{9,25},{17,1},{25,9},{2,18},{10... | collective-permute-start | bytes 1572872 | tf_op jit(solution)/shard_map/ppermute | solution.py:164
  83.6 13.4 %collective-permute-start.18 = (bf16[512,512]{1,0:T(8,128)(2,1)}, bf16[512,512]{1,0:T(8,128)(2,1)}, u32[]{:S(2)}, u32[]{:S(2)}) collective-permute-start(bf16[512,512]{1,0:T(8,128)(2,1)} %collective-permute-done.17.refs_6_), channel_id=1, source_target_pairs={{0,6},{1,7},{2,0},{3,1},{4,2},{5,3},{6,4},{7,5},{8,14},{9,15},{10,... | collective-permute-start | bytes 1572872 | tf_op jit(solution)/shard_map/ppermute | solution.py:156
  89.1 18.9 %collective-permute-start.22 = (bf16[512,512]{1,0:T(8,128)(2,1)}, bf16[512,512]{1,0:T(8,128)(2,1)}, u32[]{:S(2)}, u32[]{:S(2)}) collective-permute-start(bf16[512,512]{1,0:T(8,128)(2,1)} %collective-permute-done.17.refs_6_), channel_id=1, source_target_pairs={{0,16},{8,24},{16,0},{24,8},{1,17},{9,25},{17,1},{25,9},{2,18},{10... | collective-permute-start | bytes 1572872 | tf_op jit(solution)/shard_map/ppermute | solution.py:164
  90.6 17.4 %collective-permute-start.23 = (bf16[512,512]{1,0:T(8,128)(2,1)}, bf16[512,512]{1,0:T(8,128)(2,1)}, u32[]{:S(2)}, u32[]{:S(2)}) collective-permute-start(bf16[512,512]{1,0:T(8,128)(2,1)} %collective-permute-done.17.refs_6_), channel_id=1, source_target_pairs={{0,1},{1,0},{2,3},{3,2},{4,5},{5,4},{6,7},{7,6},{8,9},{9,8},{10,11... | collective-permute-start | bytes 1572872 | tf_op jit(solution)/shard_map/ppermute | solution.py:168
  90.6 17.7 %collective-permute-start.25 = (bf16[512,512]{1,0:T(8,128)(2,1)}, bf16[512,512]{1,0:T(8,128)(2,1)}, u32[]{:S(2)}, u32[]{:S(2)}) collective-permute-start(bf16[512,512]{1,0:T(8,128)(2,1)} %collective-permute-done.10.refs_10_), channel_id=1, source_target_pairs={{0,1},{1,0},{2,3},{3,2},{4,5},{5,4},{6,7},{7,6},{8,9},{9,8},{10,11... | collective-permute-start | bytes 1572872 | tf_op jit(solution)/shard_map/ppermute | solution.py:168
  97.0 21.1 %collective-permute-start.11 = (bf16[512,512]{1,0:T(8,128)(2,1)}, bf16[512,512]{1,0:T(8,128)(2,1)}, u32[]{:S(2)}, u32[]{:S(2)}) collective-permute-start(bf16[512,512]{1,0:T(8,128)(2,1)} %collective-permute-done.10.refs_10_), channel_id=1, source_target_pairs={{0,6},{1,7},{2,0},{3,1},{4,2},{5,3},{6,4},{7,5},{8,14},{9,15},{10,... | collective-permute-start | bytes 1572872 | tf_op jit(solution)/shard_map/ppermute | solution.py:156
  101.3 17.2 %collective-permute-start.19 = (bf16[512,512]{1,0:T(8,128)(2,1)}, bf16[512,512]{1,0:T(8,128)(2,1)}, u32[]{:S(2)}, u32[]{:S(2)}) collective-permute-start(bf16[512,512]{1,0:T(8,128)(2,1)} %collective-permute-done.18.refs_6_), channel_id=1, source_target_pairs={{0,16},{8,24},{16,0},{24,8},{1,17},{9,25},{17,1},{25,9},{2,18},{10... | collective-permute-start | bytes 1572872 | tf_op jit(solution)/shard_map/ppermute | solution.py:164
  108.0 20.7 %collective-permute-start.26 = (bf16[512,512]{1,0:T(8,128)(2,1)}, bf16[512,512]{1,0:T(8,128)(2,1)S(1)}, u32[]{:S(2)}, u32[]{:S(2)}) collective-permute-start(bf16[512,512]{1,0:T(8,128)(2,1)} %collective-permute-done.12.refs_11_), channel_id=1, source_target_pairs={{0,1},{1,0},{2,3},{3,2},{4,5},{5,4},{6,7},{7,6},{8,9},{9,8},{10,11... | collective-permute-start | bytes 1572872 | tf_op jit(solution)/shard_map/ppermute | solution.py:168
  108.1 21.0 %collective-permute-start.13 = (bf16[512,512]{1,0:T(8,128)(2,1)}, bf16[512,512]{1,0:T(8,128)(2,1)S(1)}, u32[]{:S(2)}, u32[]{:S(2)}) collective-permute-start(bf16[512,512]{1,0:T(8,128)(2,1)} %collective-permute-done.12.refs_11_), channel_id=1, source_target_pairs={{0,6},{1,7},{2,0},{3,1},{4,2},{5,3},{6,4},{7,5},{8,14},{9,15},{10,... | collective-permute-start | bytes 1572872 | tf_op jit(solution)/shard_map/ppermute | solution.py:162
  108.3 21.0 %collective-permute-start.24 = (bf16[512,512]{1,0:T(8,128)(2,1)}, bf16[512,512]{1,0:T(8,128)(2,1)S(1)}, u32[]{:S(2)}, u32[]{:S(2)}) collective-permute-start(bf16[512,512]{1,0:T(8,128)(2,1)} %collective-permute-done.22.refs_7_), channel_id=1, source_target_pairs={{0,1},{1,0},{2,3},{3,2},{4,5},{5,4},{6,7},{7,6},{8,9},{9,8},{10,11... | collective-permute-start | bytes 1572872 | tf_op jit(solution)/shard_map/ppermute | solution.py:168
  118.1 22.0 %collective-permute-start.20 = (bf16[512,512]{1,0:T(8,128)(2,1)}, bf16[512,512]{1,0:T(8,128)(2,1)S(1)}, u32[]{:S(2)}, u32[]{:S(2)}) collective-permute-start(bf16[512,512]{1,0:T(8,128)(2,1)} %collective-permute-done.18.refs_6_), channel_id=1, source_target_pairs={{0,1},{1,0},{2,3},{3,2},{4,5},{5,4},{6,7},{7,6},{8,9},{9,8},{10,11... | collective-permute-start | bytes 1572872 | tf_op jit(solution)/shard_map/ppermute | solution.py:168
  118.5 21.6 %collective-permute-start.21 = (bf16[512,512]{1,0:T(8,128)(2,1)}, bf16[512,512]{1,0:T(8,128)(2,1)S(1)}, u32[]{:S(2)}, u32[]{:S(2)}) collective-permute-start(bf16[512,512]{1,0:T(8,128)(2,1)} %collective-permute-done.19.refs_7_), channel_id=1, source_target_pairs={{0,1},{1,0},{2,3},{3,2},{4,5},{5,4},{6,7},{7,6},{8,9},{9,8},{10,11... | collective-permute-start | bytes 1572872 | tf_op jit(solution)/shard_map/ppermute | solution.py:168
  128.7 19.6 %collective-permute-start.14 = (bf16[512,512]{1,0:T(8,128)(2,1)}, bf16[512,512]{1,0:T(8,128)(2,1)S(1)}, u32[]{:S(2)}, u32[]{:S(2)}) collective-permute-start(bf16[512,512]{1,0:T(8,128)(2,1)} %collective-permute-done.11.refs_6_), channel_id=1, source_target_pairs={{0,1},{1,0},{2,3},{3,2},{4,5},{5,4},{6,7},{7,6},{8,9},{9,8},{10,11... | collective-permute-start | bytes 1572872 | tf_op jit(solution)/shard_map/ppermute | solution.py:168
  129.1 19.3 %collective-permute-start.15 = (bf16[512,512]{1,0:T(8,128)(2,1)S(1)}, bf16[512,512]{1,0:T(8,128)(2,1)S(1)}, u32[]{:S(2)}, u32[]{:S(2)}) collective-permute-start(bf16[512,512]{1,0:T(8,128)(2,1)S(1)} %collective-permute-done.13.refs_7_), channel_id=1, source_target_pairs={{0,1},{1,0},{2,3},{3,2},{4,5},{5,4},{6,7},{7,6},{8,9},{9,8},{10,11... | collective-permute-start | bytes 1572872 | tf_op jit(solution)/shard_map/ppermute | solution.py:168
  156.4 29.4 %collective-permute-start.33 = (bf16[512,512]{1,0:T(8,128)(2,1)}, bf16[512,512]{1,0:T(8,128)(2,1)S(1)}, u32[]{:S(2)}, u32[]{:S(2)}) collective-permute-start(bf16[512,512]{1,0:T(8,128)(2,1)} %get-tuple-element.43), channel_id=1, source_target_pairs={{0,16},{8,24},{16,0},{24,8},{1,17},{9,25},{17,1},{25,9},{2,18},{10... | collective-permute-start | bytes 1572872 | tf_op jit(solution)/shard_map/ppermute | solution.py:213
  157.0 28.8 %collective-permute-start.34 = (bf16[512,512]{1,0:T(8,128)(2,1)}, bf16[512,512]{1,0:T(8,128)(2,1)S(1)}, u32[]{:S(2)}, u32[]{:S(2)}) collective-permute-start(bf16[512,512]{1,0:T(8,128)(2,1)} %get-tuple-element.44), channel_id=1, source_target_pairs={{0,24},{8,16},{16,8},{24,0},{1,25},{9,17},{17,9},{25,1},{2,26},{10... | collective-permute-start | bytes 1572872 | tf_op jit(solution)/shard_map/ppermute | solution.py:211
  157.0 28.8 %collective-permute-start.35 = (bf16[512,512]{1,0:T(8,128)(2,1)}, bf16[512,512]{1,0:T(8,128)(2,1)S(1)}, u32[]{:S(2)}, u32[]{:S(2)}) collective-permute-start(bf16[512,512]{1,0:T(8,128)(2,1)} %get-tuple-element.46), channel_id=1, source_target_pairs={{0,8},{8,0},{16,24},{24,16},{1,9},{9,1},{17,25},{25,17},{2,10},{10... | collective-permute-start | bytes 1572872 | tf_op jit(solution)/shard_map/ppermute | solution.py:211
  (27 other events, 326.6 us)
where the time goes:
time: 190 us; the launch traced here: 189 us
  starting transfers between devices  58.5 us (31%)
  Pallas kernels  45.2 us (24%)
  waiting for transfers between devices  30.6 us (16%)
  blocking collectives  18.1 us (10%)
  other arithmetic  16.7 us (9%)
  local copies, waits for them, and re-layouts  15.6 us (8%)
  between operations  4.28 us (2%)
    pallas_call x5, Pallas kernels, slot_call(): pl.pallas_call(functools.partial(slot_kernel, part_count, halves, first),...  43.8 us
    ppermute x16, starting transfers between devices, all_parts(): return mine + [lax.ppermute(part, 'occ', other_core) for part in mine]  22.5 us
    psum x1, blocking collectives, per_device(): energies = lax.psum(energies, 'aux')  18.1 us
    ppermute x7, waiting for transfers between devices, per_device(): lax.ppermute(held[k][h], 'aux', to_chip(-dy, 0))  16.7 us
    ppermute x6, starting transfers between devices, per_device(): held.append([lax.ppermute(held[k - 1][h], 'occ', down) for h in halves])  16.3 us
    ppermute x6, waiting for transfers between devices, per_device(): held.append([lax.ppermute(held[k - 1][h], 'occ', down) for h in halves])  13.8 us
    ppermute x7, starting transfers between devices, per_device(): lax.ppermute(held[k][h], 'aux', to_chip(-dy, 0))  10.7 us
    unnamed x48, local copies, waits for them, and re-layouts  5.88 us
  transfers between devices with their start and end apart: 36, of which 6 were waited for; matrix products, arithmetic and copies ran while one was open for 11% of the time, Pallas kernels for 20%

commit v1 on v0

v1 whole, which is shorter than its diff:
```python
import functools

import jax
import jax.numpy as jnp
from jax import lax
from jax.experimental import pallas as pl
from jax.experimental.pallas import tpu as pltpu
from jax.sharding import PartitionSpec as P


LANES = 128
HALVES = 2


def levels_kernel(table, index, out):
    wanted = index[...]
    lane, row = wanted % LANES, wanted // LANES
    for col in range(wanted.shape[1] // LANES):
        cols = slice(col * LANES, (col + 1) * LANES)
        found = jnp.zeros((wanted.shape[0], LANES), jnp.float32)
        for r in range(table.shape[0]):
            line = jnp.broadcast_to(table[r : r + 1, :], found.shape)
            hit = jnp.take_along_axis(line, lane[:, cols], axis=1)
            found = jnp.where(row[:, cols] == r, hit, found)
        out[:, cols] = found


def slot_kernel(part_count, halves, first, slot, step, block, flags, *refs):
    rows_t = refs[:part_count]
    row_denom, col_denom = refs[part_count : part_count + 2]
    rest = refs[part_count + 2 :]
    parts = [rest[h * part_count : (h + 1) * part_count] for h in range(halves)]
    rest = rest[halves * part_count :]
    acc_in, energy_in = None, None
    if not first:
        acc_in, energy_in, rest = rest[:part_count], rest[part_count], rest[part_count + 1 :]
    accs, energy = rest[:part_count], rest[part_count]
    width = parts[0][0].shape[1]
    times = flags[slot].astype(jnp.float32)
    crossed = flags[flags.shape[0] - 1] != 0
    energy_sum = None
    for start in range(0, rows_t[0].shape[0], block):
        span = slice(start, start + block)
        amplitudes = []
        for h in range(halves):
            integrals = None
            for p in range(part_count):
                term = jnp.dot(rows_t[p][span, :], parts[h][p][...], preferred_element_type=jnp.float32)
                integrals = term if integrals is None else integrals + term
            denom = row_denom[span, :] + col_denom[:, h * width : (h + 1) * width]
            amplitude = (integrals / denom).astype(jnp.bfloat16)
            energy_row = jnp.sum(amplitude.astype(jnp.float32) * integrals, axis=0, keepdims=True)
            energy_sum = energy_row if energy_sum is None else energy_sum + energy_row
            amplitudes.append(amplitude)
        for j in range(part_count):
            other = (j + part_count // 2) % part_count
            term = None
            for h in range(halves):
                block_j = jnp.where(crossed, parts[h][other][...], parts[h][j][...])
                product = lax.dot_general(
                    block_j, amplitudes[h], (((1,), (1,)), ((), ())), preferred_element_type=jnp.float32
                )
                term = product if term is None else term + product
            term = times * term
            if not first:
                term = acc_in[j][:, span] + term
            accs[j][:, span] = term.astype(accs[j].dtype)
    energy[...] = jnp.zeros_like(energy) if first else energy_in[...]
    energy[step : step + 1, :] = energy_sum


def slot_call(flags, slot, step, steps, rows_t, row_denom, col_denom, parts, carry, last):
    halves, part_count = len(parts), len(parts[0])
    depth, width = parts[0][0].shape
    rows = rows_t[0].shape[0]
    first = carry is None
    operands = list(rows_t) + [row_denom, col_denom] + [part for half in parts for part in half]
    aliases = {}
    if not first:
        if not last:
            aliases = {1 + len(operands) + p: p for p in range(part_count + 1)}
        operands += list(carry)
    kinds = [jnp.float32] * part_count
    if last:
        kinds = [jnp.float32] + [jnp.bfloat16] * (part_count - 1)
    in_vmem = pl.BlockSpec(memory_space=pltpu.VMEM)
    return pl.pallas_call(
        functools.partial(slot_kernel, part_count, halves, first, slot, step, min(256, rows)),
        in_specs=[pl.BlockSpec(memory_space=pltpu.SMEM)] + [in_vmem] * len(operands),
        out_specs=[in_vmem] * (part_count + 1),
        out_shape=[jax.ShapeDtypeStruct((depth, rows), kind) for kind in kinds]
        + [jax.ShapeDtypeStruct((steps, width), jnp.float32)],
        input_output_aliases=aliases,
        compiler_params=pltpu.CompilerParams(vmem_limit_bytes=24 * 1024 * 1024),
        cost_estimate=pl.CostEstimate(
            flops=4 * rows * halves * width * depth * part_count,
            bytes_accessed=2 * part_count * depth * (halves * width + rows) + 8 * part_count * depth * rows,
            transcendentals=0,
        ),
        name="slot",
    )(flags, *operands)


def per_device(three_index, pair_list, pair_counts, domains, pao_energy, occ_energy):
    aux_local, occ_dev, dom_width = three_index.shape
    pair_rows = occ_dev * dom_width
    width = pair_rows // HALVES
    block_count = lax.axis_size("occ")
    block_id = lax.axis_index("occ")
    aux_count = lax.axis_size("aux")
    aux_rank = lax.axis_index("aux")
    slot_total = pair_list.shape[1]
    layers = block_count // 2
    rings = aux_count // 2
    rows = pair_rows // rings
    layer, core = block_id // 2, block_id % 2
    ring, side = aux_rank // 2, aux_rank % 2
    crossed = (core != side).astype(jnp.int32)
    axes = ("aux", "occ")

    def flat(y, x, z, c):
        return (y * 2 + x) * block_count + z * 2 + c

    everyone = [
        (y, x, z, c) for y in range(rings) for x in range(2) for z in range(layers) for c in range(2)
    ]
    swap = [
        (flat(y, x, z, c), flat(y, x, z, c) if c == x else flat(y, 1 - x, z, 1 - c)) for y, x, z, c in everyone
    ]
    lend = [(flat(y, x, z, c), flat(y, x, z, c) if c == x else flat(y, 1 - x, z, 1 - c)) for y, x, z, c in everyone]
    down = [(i, (i - 2) % block_count) for i in range(block_count)]
    other_core = [(i, i ^ 1) for i in range(block_count)]

    def to_chip(dy, dx):
        return [(y * 2 + x, ((y + dy) % rings) * 2 + (x ^ dx)) for y in range(rings) for x in range(2)]

    halves = range(HALVES)
    own_block = [
        three_index[:, h * occ_dev // HALVES : (h + 1) * occ_dev // HALVES].reshape(aux_local, width) for h in halves
    ]
    held = [[lax.ppermute(own_block[h], axes, swap) for h in halves]]
    for k in range(1, layers):
        held.append([lax.ppermute(held[k - 1][h], "occ", down) for h in halves])
    turned = []
    for k in range(layers):
        turned.append([])
        for h in halves:
            if k == layers - 1 and h == HALVES - 1:
                turned[k].append([lax.ppermute(part, "occ", down) for part in turned[k - 1][h]])
            else:
                turned[k].append([lax.ppermute(held[k][h], "aux", to_chip(-dy, 0)) for dy in range(1, rings)])

    def all_parts(k, h):
        mine = [held[k][h]] + turned[k][h]
        return mine + [lax.ppermute(part, "occ", other_core) for part in mine]

    levels = pl.pallas_call(
        levels_kernel, out_shape=jax.ShapeDtypeStruct(domains.shape, jnp.float32), name="levels"
    )(pao_energy.reshape(-1, LANES), domains)
    occ_levels = occ_energy.reshape(block_count, occ_dev)
    denoms = (levels[:, None, :] - occ_levels[:, :, None]).reshape(block_count, pair_rows)
    row_denom = lax.dynamic_slice(denoms, (block_id, ring * rows), (1, rows)).reshape(rows, 1)
    my_pairs = pair_list[block_id]
    valid = jnp.arange(slot_total, dtype=jnp.int32) < pair_counts[block_id]

    partner_ids = 2 * ((layer + jnp.arange(layers, dtype=jnp.int32)) % layers) + side
    hits = (my_pairs[None, :] == partner_ids[:, None]) & valid[None, :]
    flags = jnp.concatenate([jnp.sum(hits.astype(jnp.int32), axis=1), crossed[None]])

    start = ring * rows
    parts = [all_parts(0, h) for h in halves]
    rows_t = []
    for p in range(aux_count):
        other = (p + rings) % aux_count
        choices = [jnp.where(crossed == 0, parts[h][p], parts[h][other]) for h in halves]
        piece = jnp.where(start < width, choices[0], choices[1])
        piece = lax.dynamic_slice(piece, (0, start % width), (aux_local, rows))
        rows_t.append(lax.ppermute(piece, axes, lend).T)

    steps = layers - 1 + HALVES
    carry, step_slots = None, []
    for k in range(layers):
        if k > 0:
            parts = [all_parts(k, h) for h in halves]
        col_denom = lax.dynamic_slice(denoms, (2 * ((layer + k) % layers) + side, 0), (1, pair_rows))
        if k < layers - 1:
            pieces = [(parts, col_denom)]
        else:
            pieces = [([parts[h]], col_denom[:, h * width : (h + 1) * width]) for h in halves]
        for step_parts, step_denom in pieces:
            step = len(step_slots)
            step_slots.append(k)
            carry = slot_call(
                flags, k, step, steps, rows_t, row_denom, step_denom, step_parts, carry, step == steps - 1
            )
    accs, energy = carry[:aux_count], carry[aux_count]

    slices = []
    for dy in range(rings):
        near, far = accs[dy], lax.ppermute(accs[rings + dy], "aux", to_chip(dy, 1))
        if dy > 0:
            near = lax.ppermute(near, "aux", to_chip(dy, 0))
        slices.append((near.astype(jnp.float32) + far.astype(jnp.float32)).astype(jnp.bfloat16))
    step_energy = jnp.sum(energy, axis=1) / (pair_rows * pair_rows)
    step_hits = jnp.stack([hits[k] for k in step_slots])
    energies = jnp.sum(jnp.where(step_hits, step_energy[:, None], 0.0), axis=0)
    shares = [lax.ppermute(energies, "aux", to_chip(dy, dx)) for dy in range(rings) for dx in range(2) if dy or dx]
    energies = sum(shares, energies)
    ordered = []
    for i in range(rings):
        chosen = slices[0]
        for dy in range(1, rings):
            chosen = jnp.where((ring - i) % rings == dy, slices[dy], chosen)
        ordered.append(chosen)
    density_out = jnp.concatenate(ordered, axis=1)
    return (density_out.reshape(aux_local, occ_dev, dom_width), energies[None])


def solution(mesh):
    placed = (P("aux", "occ", None), P(), P(), P(), P(), P())

    return jax.shard_map(
        per_device,
        mesh=mesh,
        in_specs=placed,
        out_specs=(P("aux", "occ", None), P("occ", None)),
        check_vma=False,
    )
```

time: 190 us -> 197 us (1.037)
  waiting for transfers between devices: 30.6 us -> 58.8 us
  blocking collectives: 18.1 us -> 0 us
  starting transfers between devices: 58.5 us -> 76.2 us
  Pallas kernels: 45.2 us -> 29 us
  other arithmetic: 16.7 us -> 5.21 us
  local copies, waits for them, and re-layouts: 15.6 us -> 25.3 us
  between operations: 4.28 us -> 1.09 us
    ppermute x1 -> x7, waiting for transfers between devices: 0.01 us -> 26.8 us  [the longest x3 26.8 us: per_device(): lax.ppermute(energies, 'aux', to_chip(dy, dx))]
    psum x1 -> x0, blocking collectives: 18.1 us -> none  [per_device(): energies = lax.psum(energies, 'aux')]
    pallas_call x5, Pallas kernels: 43.8 us -> 27.6 us  [slot_call(): pl.pallas_call(functools.partial(slot_kernel, part_count, halves, first,...]
    ppermute x1 -> x7, starting transfers between devices: 2.24 us -> 14.6 us  [the longest x4 13.7 us: per_device(): rows_t.append(lax.ppermute(piece, axes, lend).T)]
    unnamed x48 -> x72, local copies, waits for them, and re-layouts: 5.88 us -> 14.8 us
    reduce_sum x6 -> x3, other arithmetic: 5.81 us -> 0.39 us  [the longest x1 0.18 us: per_device(): jnp.sum(hits.astype(jnp.int32), axis=1)]
    ppermute x6, starting transfers between devices: 16.3 us -> 21.6 us  [per_device(): held.append([lax.ppermute(held[k - 1][h], 'occ', down) for h in halves])]
    another operation x4 -> x0, other arithmetic: 4.98 us -> none  [per_device(): flags = jnp.stack([jnp.sum(hits.astype(jnp.int32)), crossed])]
  transfers between devices with their start and end apart: 36 -> 42, of which waited for: 6 -> 8; matrix products, arithmetic and copies ran while one was open for 11% -> 5% of each run, Pallas kernels for 20% -> 13%
where the time goes in v1:
time: 197 us; the launch traced here: 196 us
  starting transfers between devices  76.2 us (39%)
  waiting for transfers between devices  58.8 us (30%)
  Pallas kernels  29 us (15%)
  local copies, waits for them, and re-layouts  25.3 us (13%)
  other arithmetic  5.21 us (3%)
    pallas_call x5, Pallas kernels, slot_call(): pl.pallas_call(functools.partial(slot_kernel, part_count, halves, first,...  27.6 us
    ppermute x3, waiting for transfers between devices, per_device(): lax.ppermute(energies, 'aux', to_chip(dy, dx))  26.8 us
    ppermute x16, starting transfers between devices, all_parts(): return mine + [lax.ppermute(part, 'occ', other_core) for part in mine]  23 us
    ppermute x6, starting transfers between devices, per_device(): held.append([lax.ppermute(held[k - 1][h], 'occ', down) for h in halves])  21.6 us
    ppermute x7, waiting for transfers between devices, per_device(): lax.ppermute(held[k][h], 'aux', to_chip(-dy, 0))  19.9 us
    unnamed x72, local copies, waits for them, and re-layouts  14.8 us
    ppermute x4, starting transfers between devices, per_device(): rows_t.append(lax.ppermute(piece, axes, lend).T)  13.7 us
    ppermute x6, waiting for transfers between devices, per_device(): held.append([lax.ppermute(held[k - 1][h], 'occ', down) for h in halves])  12 us
  transfers between devices with their start and end apart: 42, of which 8 were waited for; matrix products, arithmetic and copies ran while one was open for 5% of the time, Pallas kernels for 13%

profile of v1, /device:TPU:0, one launch (start us, length us, event | category | flops | bytes accessed | tf_op | source)
XLA Modules:
  0.0 195.6 jit_solution(16643525913515716812)
XLA Ops:
  0.6 2.5 %fusion.4 = (bf16[512,2,256]{2,1,0:T(2,128)(2,1)S(1)}, bf16[512,2,256]{2,1,0:T(2,128)(2,1)S(1)}) fusion(bf16[512,4,256]{2,1,0:T(4,128)(2,1)} %param.6), kind=kLoop, calls=%fused_computation.30 | loop fusion | bytes 2097152 | tf_op jit(solution)/shard_map/slice | solution.py:139
  6.5 3.1 %collective-permute-start.5 = (bf16[512,512]{1,0:T(8,128)(2,1)S(1)}, bf16[512,512]{1,0:T(8,128)(2,1)S(1)}, u32[]{:S(2)}, u32[]{:S(2)}) collective-permute-start(bf16[512,512]{1,0:T(8,128)(2,1)S(1)} %collective-permute-done.refs_6_), channel_id=1, source_target_pairs={{0,16},{8,24},{16,0},{24,8},{1,17},{9,25},{17,1},{25,9},{2,18},{10... | collective-permute-start | bytes 1572872 | tf_op jit(solution)/shard_map/ppermute | solution.py:151
  9.7 13.4 %collective-permute-start.1 = (bf16[512,512]{1,0:T(8,128)(2,1)S(1)}, bf16[512,512]{1,0:T(8,128)(2,1)S(1)}, u32[]{:S(2)}, u32[]{:S(2)}) collective-permute-start(bf16[512,512]{1,0:T(8,128)(2,1)S(1)} %collective-permute-done.refs_6_), channel_id=1, source_target_pairs={{0,1},{1,0},{2,3},{3,2},{4,5},{5,4},{6,7},{7,6},{8,9},{9,8},{10,11... | collective-permute-start | bytes 1572872 | tf_op jit(solution)/shard_map/ppermute | solution.py:155
  23.2 3.6 %collective-permute-start.19 = (bf16[512,512]{1,0:T(8,128)(2,1)S(1)}, bf16[512,512]{1,0:T(8,128)(2,1)}, u32[]{:S(2)}, u32[]{:S(2)}) collective-permute-start(bf16[512,512]{1,0:T(8,128)(2,1)S(1)} %collective-permute-done.refs_6_), channel_id=1, source_target_pairs={{0,6},{1,7},{2,0},{3,1},{4,2},{5,3},{6,4},{7,5},{8,14},{9,15},{10,... | collective-permute-start | bytes 1572872 | tf_op jit(solution)/shard_map/ppermute | solution.py:143
  27.2 6.6 %collective-permute-start.6 = (bf16[512,512]{1,0:T(8,128)(2,1)S(1)}, bf16[512,512]{1,0:T(8,128)(2,1)S(1)}, u32[]{:S(2)}, u32[]{:S(2)}) collective-permute-start(bf16[512,512]{1,0:T(8,128)(2,1)S(1)} %collective-permute-done.5.refs_7_), channel_id=1, source_target_pairs={{0,1},{1,0},{2,3},{3,2},{4,5},{5,4},{6,7},{7,6},{8,9},{9,8},{10,11... | collective-permute-start | bytes 1572872 | tf_op jit(solution)/shard_map/ppermute | solution.py:155
  34.8 1.4 collective-permute-start.10
  36.3 2.8 %collective-permute-done.19.refs_6_ = bf16[512,512]{1,0:T(8,128)(2,1)} collective-permute-done((bf16[512,512]{1,0:T(8,128)(2,1)S(1)}, bf16[512,512]{1,0:T(8,128)(2,1)}, u32[]{:S(2)}, u32[]{:S(2)}) %collective-permute-start.19) | collective-permute-done | bytes 524320 | tf_op jit(solution)/shard_map/ppermute | solution.py:143
  39.1 1.6 collective-permute-start.4
  40.6 9.2 %collective-permute-done.12.refs_10_ = bf16[512,512]{1,0:T(8,128)(2,1)} collective-permute-done((bf16[512,512]{1,0:T(8,128)(2,1)S(1)}, bf16[512,512]{1,0:T(8,128)(2,1)}, u32[]{:S(2)}, u32[]{:S(2)}) %collective-permute-start.12) | collective-permute-done | bytes 524320 | tf_op jit(solution)/shard_map/ppermute | solution.py:143
  50.4 1.5 collective-permute-start.33
  52.4 4.4 %collective-permute-start.13 = (bf16[512,512]{1,0:T(8,128)(2,1)}, bf16[512,512]{1,0:T(8,128)(2,1)}, u32[]{:S(2)}, u32[]{:S(2)}) collective-permute-start(bf16[512,512]{1,0:T(8,128)(2,1)} %collective-permute-done.12.refs_10_), channel_id=1, source_target_pairs={{0,6},{1,7},{2,0},{3,1},{4,2},{5,3},{6,4},{7,5},{8,14},{9,15},{10,... | collective-permute-start | bytes 1572872 | tf_op jit(solution)/shard_map/ppermute | solution.py:143
  58.0 6.9 %collective-permute-done.30.refs_7_ = bf16[512,512]{1,0:T(8,128)(2,1)S(1)} collective-permute-done((bf16[512,512]{1,0:T(8,128)(2,1)}, bf16[512,512]{1,0:T(8,128)(2,1)S(1)}, u32[]{:S(2)}, u32[]{:S(2)}) %collective-permute-start.30) | collective-permute-done | bytes 524320 | tf_op jit(solution)/shard_map/ppermute | solution.py:151
  64.9 4.4 %collective-permute-start.20 = (bf16[512,512]{1,0:T(8,128)(2,1)}, bf16[512,512]{1,0:T(8,128)(2,1)}, u32[]{:S(2)}, u32[]{:S(2)}) collective-permute-start(bf16[512,512]{1,0:T(8,128)(2,1)} %collective-permute-done.19.refs_6_), channel_id=1, source_target_pairs={{0,6},{1,7},{2,0},{3,1},{4,2},{5,3},{6,4},{7,5},{8,14},{9,15},{10,... | collective-permute-start | bytes 1572872 | tf_op jit(solution)/shard_map/ppermute | solution.py:143
  69.2 5.5 %collective-permute-done.33.refs_11_ = bf16[512,512]{1,0:T(8,128)(2,1)S(1)} collective-permute-done((bf16[512,512]{1,0:T(8,128)(2,1)}, bf16[512,512]{1,0:T(8,128)(2,1)S(1)}, u32[]{:S(2)}, u32[]{:S(2)}) %collective-permute-start.33) | collective-permute-done | bytes 524320 | tf_op jit(solution)/shard_map/ppermute | solution.py:151
  74.8 5.4 %collective-permute-start.9 = (bf16[512,512]{1,0:T(8,128)(2,1)}, bf16[512,512]{1,0:T(8,128)(2,1)}, u32[]{:S(2)}, u32[]{:S(2)}) collective-permute-start(bf16[512,512]{1,0:T(8,128)(2,1)} %get-tuple-element.57), channel_id=1, source_target_pairs={{0,0},{1,8},{2,2},{3,10},{4,4},{5,12},{6,6},{7,14},{8,1},{9,9},{10... | collective-permute-start | bytes 1572872 | tf_op jit(solution)/shard_map/ppermute | solution.py:178
  80.3 1.4 levels.1
  83.2 5.4 %collective-permute-start.11 = (bf16[512,512]{1,0:T(8,128)(2,1)}, bf16[512,512]{1,0:T(8,128)(2,1)}, u32[]{:S(2)}, u32[]{:S(2)}) collective-permute-start(bf16[512,512]{1,0:T(8,128)(2,1)} %get-tuple-element.56), channel_id=1, source_target_pairs={{0,0},{1,8},{2,2},{3,10},{4,4},{5,12},{6,6},{7,14},{8,1},{9,9},{10... | collective-permute-start | bytes 1572872 | tf_op jit(solution)/shard_map/ppermute | solution.py:178
  92.8 4.4 %collective-permute-start.21 = (bf16[512,512]{1,0:T(8,128)(2,1)}, bf16[512,512]{1,0:T(8,128)(2,1)S(1)}, u32[]{:S(2)}, u32[]{:S(2)}) collective-permute-start(bf16[512,512]{1,0:T(8,128)(2,1)} %collective-permute-done.20.refs_6_), channel_id=1, source_target_pairs={{0,6},{1,7},{2,0},{3,1},{4,2},{5,3},{6,4},{7,5},{8,14},{9,15},{10,... | collective-permute-start | bytes 1572872 | tf_op jit(solution)/shard_map/ppermute | solution.py:143
  97.9 1.5 collective-permute-start.25
  100.9 6.3 %collective-permute-done.15.refs_11_ = bf16[512,512]{1,0:T(8,128)(2,1)S(1)} collective-permute-done((bf16[512,512]{1,0:T(8,128)(2,1)}, bf16[512,512]{1,0:T(8,128)(2,1)S(1)}, u32[]{:S(2)}, u32[]{:S(2)}) %collective-permute-start.15) | collective-permute-done | bytes 524320 | tf_op jit(solution)/shard_map/ppermute | solution.py:151
  107.3 4.4 %collective-permute-start.14 = (bf16[512,512]{1,0:T(8,128)(2,1)}, bf16[512,512]{1,0:T(8,128)(2,1)S(1)}, u32[]{:S(2)}, u32[]{:S(2)}) collective-permute-start(bf16[512,512]{1,0:T(8,128)(2,1)} %collective-permute-done.13.refs_10_), channel_id=1, source_target_pairs={{0,6},{1,7},{2,0},{3,1},{4,2},{5,3},{6,4},{7,5},{8,14},{9,15},{10,... | collective-permute-start | bytes 1572872 | tf_op jit(solution)/shard_map/ppermute | solution.py:143
  118.6 4.4 %collective-permute-start.16 = (bf16[512,512]{1,0:T(8,128)(2,1)}, bf16[512,512]{1,0:T(8,128)(2,1)S(1)}, u32[]{:S(2)}, u32[]{:S(2)}) collective-permute-start(bf16[512,512]{1,0:T(8,128)(2,1)} %copy-done.27), channel_id=1, source_target_pairs={{0,6},{1,7},{2,0},{3,1},{4,2},{5,3},{6,4},{7,5},{8,14},{9,15},{10,... | collective-permute-start | bytes 1572872 | tf_op jit(solution)/shard_map/ppermute | solution.py:149
  131.6 5.5 %slot.5 = (f32[512,512]{1,0:T(8,128)S(1)}, f32[512,512]{1,0:T(8,128)S(1)}, f32[512,512]{1,0:T(8,128)S(1)}, f32[512,512]{1,0:T(8,128)S(1)}, f32[5,512]{1,0:T(8,128)S(1)}) custom-call(s32[5]{0:T(128)S(1)} %pad_add_fusion.flags, bf16[512,512]{1,0:T(8,128)(2,1)S(1)} %copy.99.refs_0_, bf16[512,512]{1,0:T(8,128)(2,1)S(1)} %copy.100.refs_1_, ...), custom_call_target="tpu_custom_call" | custom-call | flops 4294967296 | bytes 14680064 | tf_op jit(solution)/shard_map/slot/pallas_call | solution.py:87
  137.7 6.6 %slot.6 = (f32[512,512]{1,0:T(8,128)S(1)}, f32[512,512]{1,0:T(8,128)S(1)}, f32[512,512]{1,0:T(8,128)S(1)}, f32[512,512]{1,0:T(8,128)S(1)}, f32[5,512]{1,0:T(8,128)S(1)}) custom-call(s32[5]{0:T(128)S(1)} %pad_add_fusion.flags, bf16[512,512]{1,0:T(8,128)(2,1)S(1)} %copy.99.refs_0_, ...), custom_call_target="tpu_custom_call", output_to_operand_aliasing={{0}: (15, {}), {1}: (16, {}), {2}: (17, {}), {3}: (18, {}),... | custom-call | flops 4294967296 | bytes 14680064 | tf_op jit(solution)/shard_map/slot/pallas_call | solution.py:87
  144.9 7.1 %slot.7 = (f32[512,512]{1,0:T(8,128)S(1)}, f32[512,512]{1,0:T(8,128)S(1)}, f32[512,512]{1,0:T(8,128)S(1)}, f32[512,512]{1,0:T(8,128)S(1)}, f32[5,512]{1,0:T(8,128)S(1)}) custom-call(s32[5]{0:T(128)S(1)} %pad_add_fusion.flags, bf16[512,512]{1,0:T(8,128)(2,1)S(1)} %copy.99.refs_0_, ...), custom_call_target="tpu_custom_call", output_to_operand_aliasing={{0}: (15, {}), {1}: (16, {}), {2}: (17, {}), {3}: (18, {}),... | custom-call | flops 4294967296 | bytes 14680064 | tf_op jit(solution)/shard_map/slot/pallas_call | solution.py:87
  152.1 4.1 %slot.8 = (f32[512,512]{1,0:T(8,128)S(1)}, f32[512,512]{1,0:T(8,128)S(1)}, f32[512,512]{1,0:T(8,128)S(1)}, f32[512,512]{1,0:T(8,128)S(1)}, f32[5,512]{1,0:T(8,128)S(1)}) custom-call(s32[5]{0:T(128)S(1)} %pad_add_fusion.flags, bf16[512,512]{1,0:T(8,128)(2,1)S(1)} %copy.99.refs_0_, ...), custom_call_target="tpu_custom_call", output_to_operand_aliasing={{0}: (11, {}), {1}: (12, {}), {2}: (13, {}), {3}: (14, {}),... | custom-call | flops 2147483648 | bytes 12582912 | tf_op jit(solution)/shard_map/slot/pallas_call | solution.py:87
  156.2 4.3 %slot.9 = (f32[512,512]{1,0:T(8,128)S(1)}, bf16[512,512]{1,0:T(8,128)(2,1)}, bf16[512,512]{1,0:T(8,128)(2,1)}, bf16[512,512]{1,0:T(8,128)(2,1)}, f32[5,512]{1,0:T(8,128)S(1)}) custom-call(s32[5]{0:T(128)S(1)} %pad_add_fusion.flags, bf16[512,512]{1,0:T(8,128)(2,1)S(1)} %copy.99.refs_0_, bf16[512,512]{1,0:T(8,128)(2,1)S(1)} %copy.100.refs_1_, ...), custom_call_target="tpu_custom_call" | custom-call | flops 2147483648 | bytes 12582912 | tf_op jit(solution)/shard_map/slot/pallas_call | solution.py:87
  161.0 3.0 %collective-permute-start.38 = (bf16[512,512]{1,0:T(8,128)(2,1)}, bf16[512,512]{1,0:T(8,128)(2,1)}, u32[]{:S(2)}, u32[]{:S(2)}) collective-permute-start(bf16[512,512]{1,0:T(8,128)(2,1)} %get-tuple-element.50), channel_id=1, source_target_pairs={{0,8},{8,0},{16,24},{24,16},{1,9},{9,1},{17,25},{25,17},{2,10},{10... | collective-permute-start | bytes 1572872 | tf_op jit(solution)/shard_map/ppermute | solution.py:200
  164.8 22.6 %collective-permute-done.39 = f32[6]{0:T(128)S(1)} collective-permute-done((f32[6]{0:T(128)S(1)}, f32[6]{0:T(128)S(1)}, u32[]{:S(2)}, u32[]{:S(2)}) %collective-permute-start.39) | collective-permute-done | bytes 56 | tf_op jit(solution)/shard_map/ppermute | solution.py:207
  187.7 4.2 %collective-permute-done.41 = f32[6]{0:T(128)S(1)} collective-permute-done((f32[6]{0:T(128)S(1)}, f32[6]{0:T(128)S(1)}, u32[]{:S(2)}, u32[]{:S(2)}) %collective-permute-start.41) | collective-permute-done | bytes 56 | tf_op jit(solution)/shard_map/ppermute | solution.py:207
  192.4 1.4 broadcast_select_fusion.1
  194.0 1.6 reshape.53
  (159 shorter events, 33.9 us)
Async XLA Ops:
  6.5 20.2 %collective-permute-start.5 = (bf16[512,512]{1,0:T(8,128)(2,1)S(1)}, bf16[512,512]{1,0:T(8,128)(2,1)S(1)}, u32[]{:S(2)}, u32[]{:S(2)}) collective-permute-start(bf16[512,512]{1,0:T(8,128)(2,1)S(1)} %collective-permute-done.refs_6_), channel_id=1, source_target_pairs={{0,16},{8,24},{16,0},{24,8},{1,17},{9,25},{17,1},{25,9},{2,18},{10... | collective-permute-start | bytes 1572872 | tf_op jit(solution)/shard_map/ppermute | solution.py:151
  9.6 17.6 %collective-permute-start.7 = (bf16[512,512]{1,0:T(8,128)(2,1)S(1)}, bf16[512,512]{1,0:T(8,128)(2,1)S(1)}, u32[]{:S(2)}, u32[]{:S(2)}) collective-permute-start(bf16[512,512]{1,0:T(8,128)(2,1)S(1)} %collective-permute-done.2.refs_10_), channel_id=1, source_target_pairs={{0,16},{8,24},{16,0},{24,8},{1,17},{9,25},{17,1},{25,9},{2,18},{10... | collective-permute-start | bytes 1572872 | tf_op jit(solution)/shard_map/ppermute | solution.py:151
  9.7 24.1 %collective-permute-start.1 = (bf16[512,512]{1,0:T(8,128)(2,1)S(1)}, bf16[512,512]{1,0:T(8,128)(2,1)S(1)}, u32[]{:S(2)}, u32[]{:S(2)}) collective-permute-start(bf16[512,512]{1,0:T(8,128)(2,1)S(1)} %collective-permute-done.refs_6_), channel_id=1, source_target_pairs={{0,1},{1,0},{2,3},{3,2},{4,5},{5,4},{6,7},{7,6},{8,9},{9,8},{10,11... | collective-permute-start | bytes 1572872 | tf_op jit(solution)/shard_map/ppermute | solution.py:155
  23.2 15.9 %collective-permute-start.19 = (bf16[512,512]{1,0:T(8,128)(2,1)S(1)}, bf16[512,512]{1,0:T(8,128)(2,1)}, u32[]{:S(2)}, u32[]{:S(2)}) collective-permute-start(bf16[512,512]{1,0:T(8,128)(2,1)S(1)} %collective-permute-done.refs_6_), channel_id=1, source_target_pairs={{0,6},{1,7},{2,0},{3,1},{4,2},{5,3},{6,4},{7,5},{8,14},{9,15},{10,... | collective-permute-start | bytes 1572872 | tf_op jit(solution)/shard_map/ppermute | solution.py:143
  26.8 23.1 %collective-permute-start.12 = (bf16[512,512]{1,0:T(8,128)(2,1)S(1)}, bf16[512,512]{1,0:T(8,128)(2,1)}, u32[]{:S(2)}, u32[]{:S(2)}) collective-permute-start(bf16[512,512]{1,0:T(8,128)(2,1)S(1)} %collective-permute-done.2.refs_10_), channel_id=1, source_target_pairs={{0,6},{1,7},{2,0},{3,1},{4,2},{5,3},{6,4},{7,5},{8,14},{9,15},{10,... | collective-permute-start | bytes 1572872 | tf_op jit(solution)/shard_map/ppermute | solution.py:143
  27.2 23.1 %collective-permute-start.6 = (bf16[512,512]{1,0:T(8,128)(2,1)S(1)}, bf16[512,512]{1,0:T(8,128)(2,1)S(1)}, u32[]{:S(2)}, u32[]{:S(2)}) collective-permute-start(bf16[512,512]{1,0:T(8,128)(2,1)S(1)} %collective-permute-done.5.refs_7_), channel_id=1, source_target_pairs={{0,1},{1,0},{2,3},{3,2},{4,5},{5,4},{6,7},{7,6},{8,9},{9,8},{10,11... | collective-permute-start | bytes 1572872 | tf_op jit(solution)/shard_map/ppermute | solution.py:155
  33.8 18.0 %collective-permute-start.8 = (bf16[512,512]{1,0:T(8,128)(2,1)S(1)}, bf16[512,512]{1,0:T(8,128)(2,1)S(1)}, u32[]{:S(2)}, u32[]{:S(2)}) collective-permute-start(bf16[512,512]{1,0:T(8,128)(2,1)S(1)} %collective-permute-done.7.refs_11_), channel_id=1, source_target_pairs={{0,1},{1,0},{2,3},{3,2},{4,5},{5,4},{6,7},{7,6},{8,9},{9,8},{10,11... | collective-permute-start | bytes 1572872 | tf_op jit(solution)/shard_map/ppermute | solution.py:155
  34.8 17.1 %collective-permute-start.10 = (bf16[512,512]{1,0:T(8,128)(2,1)S(1)}, bf16[512,512]{1,0:T(8,128)(2,1)}, u32[]{:S(2)}, u32[]{:S(2)}) collective-permute-start(bf16[512,512]{1,0:T(8,128)(2,1)S(1)} %get-tuple-element.58), channel_id=1, source_target_pairs={{0,0},{1,8},{2,2},{3,10},{4,4},{5,12},{6,6},{7,14},{8,1},{9,9},{10... | collective-permute-start | bytes 1572872 | tf_op jit(solution)/shard_map/ppermute | solution.py:178
  49.8 15.0 %collective-permute-start.30 = (bf16[512,512]{1,0:T(8,128)(2,1)}, bf16[512,512]{1,0:T(8,128)(2,1)S(1)}, u32[]{:S(2)}, u32[]{:S(2)}) collective-permute-start(bf16[512,512]{1,0:T(8,128)(2,1)} %collective-permute-done.19.refs_6_), channel_id=1, source_target_pairs={{0,16},{8,24},{16,0},{24,8},{1,17},{9,25},{17,1},{25,9},{2,18},{10... | collective-permute-start | bytes 1572872 | tf_op jit(solution)/shard_map/ppermute | solution.py:151
  50.4 24.4 %collective-permute-start.33 = (bf16[512,512]{1,0:T(8,128)(2,1)}, bf16[512,512]{1,0:T(8,128)(2,1)S(1)}, u32[]{:S(2)}, u32[]{:S(2)}) collective-permute-start(bf16[512,512]{1,0:T(8,128)(2,1)} %collective-permute-done.12.refs_10_), channel_id=1, source_target_pairs={{0,16},{8,24},{16,0},{24,8},{1,17},{9,25},{17,1},{25,9},{2,18},{10... | collective-permute-start | bytes 1572872 | tf_op jit(solution)/shard_map/ppermute | solution.py:151
  51.9 30.4 %collective-permute-start.31 = (bf16[512,512]{1,0:T(8,128)(2,1)}, bf16[512,512]{1,0:T(8,128)(2,1)S(1)}, u32[]{:S(2)}, u32[]{:S(2)}) collective-permute-start(bf16[512,512]{1,0:T(8,128)(2,1)} %collective-permute-done.19.refs_6_), channel_id=1, source_target_pairs={{0,1},{1,0},{2,3},{3,2},{4,5},{5,4},{6,7},{7,6},{8,9},{9,8},{10,11... | collective-permute-start | bytes 1572872 | tf_op jit(solution)/shard_map/ppermute | solution.py:155
  51.9 36.6 %collective-permute-start.34 = (bf16[512,512]{1,0:T(8,128)(2,1)}, bf16[512,512]{1,0:T(8,128)(2,1)S(1)}, u32[]{:S(2)}, u32[]{:S(2)}) collective-permute-start(bf16[512,512]{1,0:T(8,128)(2,1)} %collective-permute-done.12.refs_10_), channel_id=1, source_target_pairs={{0,1},{1,0},{2,3},{3,2},{4,5},{5,4},{6,7},{7,6},{8,9},{9,8},{10,11... | collective-permute-start | bytes 1572872 | tf_op jit(solution)/shard_map/ppermute | solution.py:155
  52.4 37.8 %collective-permute-start.13 = (bf16[512,512]{1,0:T(8,128)(2,1)}, bf16[512,512]{1,0:T(8,128)(2,1)}, u32[]{:S(2)}, u32[]{:S(2)}) collective-permute-start(bf16[512,512]{1,0:T(8,128)(2,1)} %collective-permute-done.12.refs_10_), channel_id=1, source_target_pairs={{0,6},{1,7},{2,0},{3,1},{4,2},{5,3},{6,4},{7,5},{8,14},{9,15},{10,... | collective-permute-start | bytes 1572872 | tf_op jit(solution)/shard_map/ppermute | solution.py:143
  64.9 27.4 %collective-permute-start.20 = (bf16[512,512]{1,0:T(8,128)(2,1)}, bf16[512,512]{1,0:T(8,128)(2,1)}, u32[]{:S(2)}, u32[]{:S(2)}) collective-permute-start(bf16[512,512]{1,0:T(8,128)(2,1)} %collective-permute-done.19.refs_6_), channel_id=1, source_target_pairs={{0,6},{1,7},{2,0},{3,1},{4,2},{5,3},{6,4},{7,5},{8,14},{9,15},{10,... | collective-permute-start | bytes 1572872 | tf_op jit(solution)/shard_map/ppermute | solution.py:143
  74.8 18.0 %collective-permute-start.9 = (bf16[512,512]{1,0:T(8,128)(2,1)}, bf16[512,512]{1,0:T(8,128)(2,1)}, u32[]{:S(2)}, u32[]{:S(2)}) collective-permute-start(bf16[512,512]{1,0:T(8,128)(2,1)} %get-tuple-element.57), channel_id=1, source_target_pairs={{0,0},{1,8},{2,2},{3,10},{4,4},{5,12},{6,6},{7,14},{8,1},{9,9},{10... | collective-permute-start | bytes 1572872 | tf_op jit(solution)/shard_map/ppermute | solution.py:178
  83.2 14.7 %collective-permute-start.11 = (bf16[512,512]{1,0:T(8,128)(2,1)}, bf16[512,512]{1,0:T(8,128)(2,1)}, u32[]{:S(2)}, u32[]{:S(2)}) collective-permute-start(bf16[512,512]{1,0:T(8,128)(2,1)} %get-tuple-element.56), channel_id=1, source_target_pairs={{0,0},{1,8},{2,2},{3,10},{4,4},{5,12},{6,6},{7,14},{8,1},{9,9},{10... | collective-permute-start | bytes 1572872 | tf_op jit(solution)/shard_map/ppermute | solution.py:178
  92.2 15.0 %collective-permute-start.15 = (bf16[512,512]{1,0:T(8,128)(2,1)}, bf16[512,512]{1,0:T(8,128)(2,1)S(1)}, u32[]{:S(2)}, u32[]{:S(2)}) collective-permute-start(bf16[512,512]{1,0:T(8,128)(2,1)} %collective-permute-done.13.refs_10_), channel_id=1, source_target_pairs={{0,16},{8,24},{16,0},{24,8},{1,17},{9,25},{17,1},{25,9},{2,18},{10... | collective-permute-start | bytes 1572872 | tf_op jit(solution)/shard_map/ppermute | solution.py:151
  92.8 18.9 %collective-permute-start.21 = (bf16[512,512]{1,0:T(8,128)(2,1)}, bf16[512,512]{1,0:T(8,128)(2,1)S(1)}, u32[]{:S(2)}, u32[]{:S(2)}) collective-permute-start(bf16[512,512]{1,0:T(8,128)(2,1)} %collective-permute-done.20.refs_6_), channel_id=1, source_target_pairs={{0,6},{1,7},{2,0},{3,1},{4,2},{5,3},{6,4},{7,5},{8,14},{9,15},{10,... | collective-permute-start | bytes 1572872 | tf_op jit(solution)/shard_map/ppermute | solution.py:143
  97.9 20.7 %collective-permute-start.25 = (bf16[512,512]{1,0:T(8,128)(2,1)}, bf16[512,512]{1,0:T(8,128)(2,1)}, u32[]{:S(2)}, u32[]{:S(2)}) collective-permute-start(bf16[512,512]{1,0:T(8,128)(2,1)} %collective-permute-done.20.refs_6_), channel_id=1, source_target_pairs={{0,16},{8,24},{16,0},{24,8},{1,17},{9,25},{17,1},{25,9},{2,18},{10... | collective-permute-start | bytes 1572872 | tf_op jit(solution)/shard_map/ppermute | solution.py:151
  99.4 19.2 %collective-permute-start.26 = (bf16[512,512]{1,0:T(8,128)(2,1)}, bf16[512,512]{1,0:T(8,128)(2,1)}, u32[]{:S(2)}, u32[]{:S(2)}) collective-permute-start(bf16[512,512]{1,0:T(8,128)(2,1)} %collective-permute-done.20.refs_6_), channel_id=1, source_target_pairs={{0,1},{1,0},{2,3},{3,2},{4,5},{5,4},{6,7},{7,6},{8,9},{9,8},{10,11... | collective-permute-start | bytes 1572872 | tf_op jit(solution)/shard_map/ppermute | solution.py:155
  100.3 22.7 %collective-permute-start.28 = (bf16[512,512]{1,0:T(8,128)(2,1)}, bf16[512,512]{1,0:T(8,128)(2,1)}, u32[]{:S(2)}, u32[]{:S(2)}) collective-permute-start(bf16[512,512]{1,0:T(8,128)(2,1)} %collective-permute-done.13.refs_10_), channel_id=1, source_target_pairs={{0,1},{1,0},{2,3},{3,2},{4,5},{5,4},{6,7},{7,6},{8,9},{9,8},{10,11... | collective-permute-start | bytes 1572872 | tf_op jit(solution)/shard_map/ppermute | solution.py:155
  107.3 29.8 %collective-permute-start.14 = (bf16[512,512]{1,0:T(8,128)(2,1)}, bf16[512,512]{1,0:T(8,128)(2,1)S(1)}, u32[]{:S(2)}, u32[]{:S(2)}) collective-permute-start(bf16[512,512]{1,0:T(8,128)(2,1)} %collective-permute-done.13.refs_10_), channel_id=1, source_target_pairs={{0,6},{1,7},{2,0},{3,1},{4,2},{5,3},{6,4},{7,5},{8,14},{9,15},{10,... | collective-permute-start | bytes 1572872 | tf_op jit(solution)/shard_map/ppermute | solution.py:143
  111.6 25.8 %collective-permute-start.22 = (bf16[512,512]{1,0:T(8,128)(2,1)S(1)}, bf16[512,512]{1,0:T(8,128)(2,1)}, u32[]{:S(2)}, u32[]{:S(2)}) collective-permute-start(bf16[512,512]{1,0:T(8,128)(2,1)S(1)} %collective-permute-done.21.refs_6_), channel_id=1, source_target_pairs={{0,16},{8,24},{16,0},{24,8},{1,17},{9,25},{17,1},{25,9},{2,18},{10... | collective-permute-start | bytes 1572872 | tf_op jit(solution)/shard_map/ppermute | solution.py:151
  118.6 25.7 %collective-permute-start.29 = (bf16[512,512]{1,0:T(8,128)(2,1)}, bf16[512,512]{1,0:T(8,128)(2,1)S(1)}, u32[]{:S(2)}, u32[]{:S(2)}) collective-permute-start(bf16[512,512]{1,0:T(8,128)(2,1)} %copy-done.27), channel_id=1, source_target_pairs={{0,1},{1,0},{2,3},{3,2},{4,5},{5,4},{6,7},{7,6},{8,9},{9,8},{10,11... | collective-permute-start | bytes 1572872 | tf_op jit(solution)/shard_map/ppermute | solution.py:155
  118.6 26.1 %collective-permute-start.16 = (bf16[512,512]{1,0:T(8,128)(2,1)}, bf16[512,512]{1,0:T(8,128)(2,1)S(1)}, u32[]{:S(2)}, u32[]{:S(2)}) collective-permute-start(bf16[512,512]{1,0:T(8,128)(2,1)} %copy-done.27), channel_id=1, source_target_pairs={{0,6},{1,7},{2,0},{3,1},{4,2},{5,3},{6,4},{7,5},{8,14},{9,15},{10,... | collective-permute-start | bytes 1572872 | tf_op jit(solution)/shard_map/ppermute | solution.py:149
  123.0 21.9 %collective-permute-start.27 = (bf16[512,512]{1,0:T(8,128)(2,1)}, bf16[512,512]{1,0:T(8,128)(2,1)S(1)}, u32[]{:S(2)}, u32[]{:S(2)}) collective-permute-start(bf16[512,512]{1,0:T(8,128)(2,1)} %collective-permute-done.25.refs_7_), channel_id=1, source_target_pairs={{0,1},{1,0},{2,3},{3,2},{4,5},{5,4},{6,7},{7,6},{8,9},{9,8},{10,11... | collective-permute-start | bytes 1572872 | tf_op jit(solution)/shard_map/ppermute | solution.py:155
  137.1 15.0 %collective-permute-start.23 = (bf16[512,512]{1,0:T(8,128)(2,1)S(1)}, bf16[512,512]{1,0:T(8,128)(2,1)S(1)}, u32[]{:S(2)}, u32[]{:S(2)}) collective-permute-start(bf16[512,512]{1,0:T(8,128)(2,1)S(1)} %collective-permute-done.21.refs_6_), channel_id=1, source_target_pairs={{0,1},{1,0},{2,3},{3,2},{4,5},{5,4},{6,7},{7,6},{8,9},{9,8},{10,11... | collective-permute-start | bytes 1572872 | tf_op jit(solution)/shard_map/ppermute | solution.py:155
  160.5 31.9 %collective-permute-start.36 = (bf16[512,512]{1,0:T(8,128)(2,1)}, bf16[512,512]{1,0:T(8,128)(2,1)S(1)}, u32[]{:S(2)}, u32[]{:S(2)}) collective-permute-start(bf16[512,512]{1,0:T(8,128)(2,1)} %get-tuple-element.47), channel_id=1, source_target_pairs={{0,16},{8,24},{16,0},{24,8},{1,17},{9,25},{17,1},{25,9},{2,18},{10... | collective-permute-start | bytes 1572872 | tf_op jit(solution)/shard_map/ppermute | solution.py:202
  161.0 31.4 %collective-permute-start.37 = (bf16[512,512]{1,0:T(8,128)(2,1)}, bf16[512,512]{1,0:T(8,128)(2,1)S(1)}, u32[]{:S(2)}, u32[]{:S(2)}) collective-permute-start(bf16[512,512]{1,0:T(8,128)(2,1)} %get-tuple-element.48), channel_id=1, source_target_pairs={{0,24},{8,16},{16,8},{24,0},{1,25},{9,17},{17,9},{25,1},{2,26},{10... | collective-permute-start | bytes 1572872 | tf_op jit(solution)/shard_map/ppermute | solution.py:200
  161.0 31.4 %collective-permute-start.38 = (bf16[512,512]{1,0:T(8,128)(2,1)}, bf16[512,512]{1,0:T(8,128)(2,1)}, u32[]{:S(2)}, u32[]{:S(2)}) collective-permute-start(bf16[512,512]{1,0:T(8,128)(2,1)} %get-tuple-element.50), channel_id=1, source_target_pairs={{0,8},{8,0},{16,24},{24,16},{1,9},{9,1},{17,25},{25,17},{2,10},{10... | collective-permute-start | bytes 1572872 | tf_op jit(solution)/shard_map/ppermute | solution.py:200
  164.2 23.2 %collective-permute-start.39 = (f32[6]{0:T(128)S(1)}, f32[6]{0:T(128)S(1)}, u32[]{:S(2)}, u32[]{:S(2)}) collective-permute-start(f32[6]{0:T(128)S(1)} %select_reduce_fusion), channel_id=1, source_target_pairs={{0,8},{8,0},{16,24},{24,16},{1,9},{9,1},{17,25},{25,17},{2,10},{10... | collective-permute-start | bytes 80 | tf_op jit(solution)/shard_map/ppermute | solution.py:207
  164.3 23.5 %collective-permute-start.40 = (f32[6]{0:T(128)S(1)}, f32[6]{0:T(128)S(1)}, u32[]{:S(2)}, u32[]{:S(2)}) collective-permute-start(f32[6]{0:T(128)S(1)} %select_reduce_fusion), channel_id=1, source_target_pairs={{0,16},{8,24},{16,0},{24,8},{1,17},{9,25},{17,1},{25,9},{2,18},{10... | collective-permute-start | bytes 80 | tf_op jit(solution)/shard_map/ppermute | solution.py:207
  (45 other events, 492.6 us)
